TPU v7x, 256 devices: a whole 4x4x8 slice. The times are simulated.
256 devices in a mesh: gx: 16 (over x_lo, y, core), yz: 16 (over z, x_hi).
Axes of the slice: x: 4 (x_hi: 2, x_lo: 2; x = x_hi * 2 + x_lo), y: 4, z: 8, core: 2. Of those that a mesh axis runs over, the one named last changes fastest.
Arguments:
- volume: bfloat16 [128, 16, 128, 128], P('gx', None, 'yz'), may hold values from -6 to 6
- weight_one: bfloat16 [32, 432], replicated, may hold values from -0.875 to 0.875
- weight_two: bfloat16 [64, 864], replicated, may hold values from -0.625 to 0.625
- weight_three: bfloat16 [128, 1728], replicated, may hold values from -0.21875 to 0.21875
Outputs:
- features: bfloat16 [128, 32, 1024], P('yz', 'gx')
All inputs are finite; a program needn't handle non-finite values.
Results may differ from a plain program's by a relative error of at most 0.0053.
Values may be sent and summed in bfloat16 or wider, within the bound.
A program may use at most 64 MiB of HBM per device.

v0:
```python
import jax
import jax.numpy as jnp
from jax import lax
from jax.sharding import PartitionSpec as P


def with_halo(block, sides, width):
    for axis, dim in sides:
        count = lax.axis_size(axis)
        forward = [(i, i + 1) for i in range(count - 1)]
        backward = [(target, source) for source, target in forward]
        low = lax.ppermute(
            lax.slice_in_dim(block, block.shape[dim] - width, None, axis=dim), axis, forward
        )
        high = lax.ppermute(lax.slice_in_dim(block, 0, width, axis=dim), axis, backward)
        block = jnp.concatenate([low, block, high], axis=dim)
    return block


def block_conv(padded, weight):
    in_rows = weight.shape[1] // 27
    kernel = weight.reshape(weight.shape[0], 3, 3, 3, in_rows)
    result = lax.conv_general_dilated(
        padded[None],
        kernel,
        (1, 1, 1),
        "VALID",
        dimension_numbers=("NDCHW", "ODHWI", "NDCHW"),
        preferred_element_type=jnp.float32,
    )
    return result[0]


def conv_pool(padded, weight):
    activated = jax.nn.relu(block_conv(padded, weight))
    planes, rows, height, breadth = activated.shape
    grouped = activated.reshape(planes // 2, 2, rows, height // 2, 2, breadth // 2, 2)
    return (jnp.sum(grouped, axis=(1, 4, 6)) * 0.125).astype(jnp.bfloat16)


def conv_planes(padded, weight):
    result = block_conv(padded, weight)
    planes, rows, height, breadth = result.shape
    return result.reshape(planes, rows, height * breadth)


def face_cells(block):
    grown = with_halo(block, (("gx", 0), ("yz", 2)), 1)
    return jnp.pad(grown, ((0, 0), (0, 0), (0, 0), (1, 1)))


def per_device(volume, weight_one, weight_two, weight_three):
    pooled_one = conv_pool(face_cells(volume), weight_one)
    pooled_two = conv_pool(face_cells(pooled_one), weight_two)
    shards = lax.axis_size("yz")
    out_rows = weight_three.shape[0] // shards
    grown = with_halo(pooled_two, (("gx", 0),), 1)
    whole = lax.all_gather(grown, "yz", axis=2, tiled=True)
    whole = jnp.pad(whole, ((0, 0), (0, 0), (1, 1), (1, 1)))
    picked = lax.dynamic_slice_in_dim(weight_three, lax.axis_index("yz") * out_rows, out_rows, 0)
    summed = jnp.moveaxis(conv_planes(whole, picked), 0, 1)
    return jax.nn.relu(summed).astype(jnp.bfloat16)


def solution(mesh):
    placed = (P("gx", None, "yz", None), P(), P(), P())
    return jax.shard_map(
        per_device, mesh=mesh, in_specs=placed, out_specs=P("yz", "gx", None), check_vma=False
    )
```

profile of v0, /device:TPU:2, one launch (start us, length us, event | category | flops | bytes accessed | tf_op | source)
XLA Modules:
  0.0 144.3 jit_solution(10215442351459870463)
XLA Ops:
  0.0 0.8 fusion.64
  0.8 1.9 %collective-permute-start = (bf16[1,16,8,128]{3,2,1,0:T(8,128)(2,1)S(1)}, bf16[1,16,8,128]{3,2,1,0:T(8,128)(2,1)S(1)}, u32[]{:S(2)}, u32[]{:S(2)}) collective-permute-start(bf16[1,16,8,128]{3,2,1,0:T(8,128)(2,1)S(1)} %get-tuple-element.12), channel_id=1, source_target_pairs={{0,16},{16,32},{32,48},{48,64},{64,80},{80,96},{96,112},{112,128},... | collective-permute-start | bytes 98312 | tf_op jit(solution)/shard_map/ppermute | solution.py:12
  2.8 5.8 %collective-permute-start.1 = (bf16[1,16,8,128]{3,2,1,0:T(8,128)(2,1)S(1)}, bf16[1,16,8,128]{3,2,1,0:T(8,128)(2,1)S(1)}, u32[]{:S(2)}, u32[]{:S(2)}) collective-permute-start(bf16[1,16,8,128]{3,2,1,0:T(8,128)(2,1)S(1)} %get-tuple-element.11), channel_id=1, source_target_pairs={{16,0},{32,16},{48,32},{64,48},{80,64},{96,80},{112,96},{128,112},... | collective-permute-start | bytes 98312 | tf_op jit(solution)/shard_map/ppermute | solution.py:15
  8.5 1.0 constant_dynamic-update-slice_fusion.1
  9.5 0.6 collective-permute-done.1
  10.2 4.0 %collective-permute-start.2 = (bf16[10,16,1,128]{3,2,1,0:T(2,128)(2,1)S(1)}, bf16[10,16,1,128]{3,2,1,0:T(2,128)(2,1)S(1)}, u32[]{:S(2)}, u32[]{:S(2)}) collective-permute-start(bf16[10,16,1,128]{3,2,1,0:T(2,128)(2,1)S(1)} %get-tuple-element.7), channel_id=1, source_target_pairs={{0,1},{1,2},{2,3},{3,4},{4,5},{5,6},{6,7},{7,8},{8,9},{9,10},{10,1... | collective-permute-start | bytes 122888 | tf_op jit(solution)/shard_map/ppermute | solution.py:12
  14.3 1.3 collective-permute-start.3
  15.6 0.9 copy.59
  16.5 5.6 %collective-permute-done.3 = bf16[10,16,1,128]{3,2,1,0:T(2,128)(2,1)S(1)} collective-permute-done((bf16[10,16,1,128]{3,2,1,0:T(2,128)(2,1)S(1)}, bf16[10,16,1,128]{3,2,1,0:T(2,128)(2,1)S(1)}, u32[]{:S(2)}, u32[]{:S(2)}) %collective-permute-start.3) | collective-permute-done | bytes 40992 | tf_op jit(solution)/shard_map/ppermute | solution.py:15
  22.1 1.2 fusion.35
  23.6 3.7 %reshape.59 = bf16[10,16,10,1,8,17]{5,4,2,1,0,3:T(8,128)(2,1)} reshape(bf16[10,16,10,1,136]{4,2,1,0,3:T(8,128)(2,1)S(1)} %pad.15) | data formatting | bytes 870400 | tf_op jit(solution)/shard_map/conv_general_dilated | solution.py:23
  27.3 7.9 %copy.58 = bf16[10,16,10,1,8,17]{1,4,5,2,0,3:T(8,128)(2,1)} copy(bf16[10,16,10,1,8,17]{5,4,2,1,0,3:T(8,128)(2,1)} %reshape.59) | data formatting | bytes 870400 | tf_op jit(solution)/shard_map/conv_general_dilated | solution.py:23
  35.2 1.1 slice.48
  36.4 7.3 %select_maximum_fusion = f32[8,8,8,17,32]{4,2,3,1,0:T(8,128)S(1)} fusion(pred[8,17]{0,1:T(8,128)(4,1)S(1)} %copy-done.2, bf16[32,3,3,3,16]{0,4,3,2,1:T(8,128)(2,1)S(1)} %bitcast.57, bf16[10,16,10,1,7,2]{1,4,5,2,0,3:T(8,128)(2,1)S(1)} %slice.48, bf16[10,16,10,1,8,17]{1,4,5,2,0,3:T(8,128)(2,1)} %copy.58), kind=kOutput, calls=%fused_computation.2 | convolution fusion | flops 242664448 | bytes 1621896 | tf_op jit(solution)/shard_map/conv_general_dilated | solution.py:23
  43.7 0.8 copy.60
  44.5 2.2 %slice.49 = f32[8,8,1,128,32]{4,1,3,0,2:T(8,128)} slice(f32[8,8,1,136,32]{4,1,3,0,2:T(8,128)S(1)} %bitcast.47), slice={[0:8], [0:8], [0:1], [0:128], [0:32]} | slice | bytes 2097152 | tf_op jit(solution)/shard_map/jit(relu)/max | solution.py:35
  46.7 5.0 %reduce_sum.18 = f32[4,32,4,64]{1,2,3,0:T(4,128)S(1)} reduce(f32[4,2,32,4,2,64,2]{2,4,3,6,5,1,0:T(2,128)} %bitcast.48, f32[]{:T(128)} %constant.8.clone.1), dimensions={1,4,6}, to_apply=%region_0.1 | reduce | flops 229376 | bytes 1179652 | tf_op jit(solution)/shard_map/reduce_sum | solution.py:38
  51.9 1.9 %collective-permute-start.4 = (bf16[1,32,4,64]{1,2,3,0:T(4,128)(2,1)S(1)}, bf16[1,32,4,64]{1,2,3,0:T(4,128)(2,1)S(1)}, u32[]{:S(2)}, u32[]{:S(2)}) collective-permute-start(bf16[1,32,4,64]{1,2,3,0:T(4,128)(2,1)S(1)} %get-tuple-element.9), channel_id=1, source_target_pairs={{0,16},{16,32},{32,48},{48,64},{64,80},{80,96},{96,112},{112,128},... | collective-permute-start | bytes 49160 | tf_op jit(solution)/shard_map/ppermute | solution.py:12
  53.8 5.8 %collective-permute-start.5 = (bf16[1,32,4,64]{1,2,3,0:T(4,128)(2,1)S(1)}, bf16[1,32,4,64]{1,2,3,0:T(4,128)(2,1)S(1)}, u32[]{:S(2)}, u32[]{:S(2)}) collective-permute-start(bf16[1,32,4,64]{1,2,3,0:T(4,128)(2,1)S(1)} %get-tuple-element.10), channel_id=1, source_target_pairs={{16,0},{32,16},{48,32},{64,48},{80,64},{96,80},{112,96},{128,112},... | collective-permute-start | bytes 49160 | tf_op jit(solution)/shard_map/ppermute | solution.py:15
  59.6 1.9 %collective-permute-done.5 = bf16[1,32,4,64]{1,2,3,0:T(4,128)(2,1)S(1)} collective-permute-done((bf16[1,32,4,64]{1,2,3,0:T(4,128)(2,1)S(1)}, bf16[1,32,4,64]{1,2,3,0:T(4,128)(2,1)S(1)}, u32[]{:S(2)}, u32[]{:S(2)}) %collective-permute-start.5) | collective-permute-done | bytes 16416 | tf_op jit(solution)/shard_map/ppermute | solution.py:15
  62.1 5.8 %collective-permute-start.6 = (bf16[6,32,1,64]{1,2,3,0:T(2,128)(2,1)S(1)}, bf16[6,32,1,64]{1,2,3,0:T(2,128)(2,1)S(1)}, u32[]{:S(2)}, u32[]{:S(2)}) collective-permute-start(bf16[6,32,1,64]{1,2,3,0:T(2,128)(2,1)S(1)} %get-tuple-element.5), channel_id=1, source_target_pairs={{0,1},{1,2},{2,3},{3,4},{4,5},{5,6},{6,7},{7,8},{8,9},{9,10},{10,1... | collective-permute-start | bytes 73736 | tf_op jit(solution)/shard_map/ppermute | solution.py:12
  67.9 1.3 collective-permute-start.7
  69.6 3.6 %collective-permute-done.6 = bf16[6,32,1,64]{1,2,3,0:T(2,128)(2,1)S(1)} collective-permute-done((bf16[6,32,1,64]{1,2,3,0:T(2,128)(2,1)S(1)}, bf16[6,32,1,64]{1,2,3,0:T(2,128)(2,1)S(1)}, u32[]{:S(2)}, u32[]{:S(2)}) %collective-permute-start.6) | collective-permute-done | bytes 24608 | tf_op jit(solution)/shard_map/ppermute | solution.py:12
  73.3 3.6 %collective-permute-done.7 = bf16[6,32,1,64]{1,2,3,0:T(2,128)(2,1)S(1)} collective-permute-done((bf16[6,32,1,64]{1,2,3,0:T(2,128)(2,1)S(1)}, bf16[6,32,1,64]{1,2,3,0:T(2,128)(2,1)S(1)}, u32[]{:S(2)}, u32[]{:S(2)}) %collective-permute-start.7) | collective-permute-done | bytes 24608 | tf_op jit(solution)/shard_map/ppermute | solution.py:15
  78.2 1.4 fusion.36
  80.3 1.9 %collective-permute-start.8 = (bf16[1,64,2,32]{1,2,3,0:T(2,128)(2,1)S(1)}, bf16[1,64,2,32]{1,2,3,0:T(2,128)(2,1)S(1)}, u32[]{:S(2)}, u32[]{:S(2)}) collective-permute-start(bf16[1,64,2,32]{1,2,3,0:T(2,128)(2,1)S(1)} %get-tuple-element.13), channel_id=1, source_target_pairs={{0,16},{16,32},{32,48},{48,64},{64,80},{80,96},{96,112},{112,128},... | collective-permute-start | bytes 24584 | tf_op jit(solution)/shard_map/ppermute | solution.py:12
  82.2 5.8 %collective-permute-start.9 = (bf16[1,64,2,32]{1,2,3,0:T(2,128)(2,1)S(1)}, bf16[1,64,2,32]{1,2,3,0:T(2,128)(2,1)S(1)}, u32[]{:S(2)}, u32[]{:S(2)}) collective-permute-start(bf16[1,64,2,32]{1,2,3,0:T(2,128)(2,1)S(1)} %get-tuple-element.14), channel_id=1, source_target_pairs={{16,0},{32,16},{48,32},{64,48},{80,64},{96,80},{112,96},{128,112},... | collective-permute-start | bytes 24584 | tf_op jit(solution)/shard_map/ppermute | solution.py:15
  88.2 1.2 collective-permute-done.9
  89.5 48.7 %all_gather.3 = bf16[4,64,32,32]{1,3,0,2:T(8,128)(2,1)S(1)} all-gather(bf16[4,64,2,32]{1,3,0,2:T(8,128)(2,1)S(1)} %copy.69), channel_id=1, replica_groups=mesh['gx'=16,'yz'=16] {'yz'}, dimensions={2}, use_global_device_ids=true | all-gather | bytes 557056 | tf_op jit(solution)/shard_map/all_gather | solution.py:58
  139.2 0.7 pad.19.clone
  140.2 2.7 %fusion.30 = bf16[2,32,8,5,8]{4,2,3,1,0:T(8,128)(2,1)S(1)} fusion(bf16[8,3,3,3,64]{0,4,3,2,1:T(8,128)(2,1)S(1)} %bitcast.54, bf16[4,64,34,1,7,2]{1,4,5,2,0,3:T(8,128)(2,1)S(1)} %slice.58, bf16[4,64,34,1,8,5]{1,4,5,2,0,3:T(8,128)(2,1)S(1)} %copy.72, pred[8,5]{0,1:T(8,128)(4,1)S(1)} %copy-done.4), kind=kOutput, calls=%fused_computation.29 | convolution fusion | flops 73764864 | bytes 1008680 | tf_op jit(solution)/shard_map/conv_general_dilated | solution.py:23
  143.6 0.7 copy.77
  (47 shorter events, 6.0 us)
Async XLA Ops:
  0.0 88.0 %copy-start = (bf16[128,1728]{0,1:T(8,128)(2,1)S(1)}, bf16[128,1728]{0,1:T(8,128)(2,1)}, u32[]{:S(2)}) copy-start(bf16[128,1728]{0,1:T(8,128)(2,1)} %param.7) | copy-start | bytes 1327108
  0.8 7.7 %collective-permute-start = (bf16[1,16,8,128]{3,2,1,0:T(8,128)(2,1)S(1)}, bf16[1,16,8,128]{3,2,1,0:T(8,128)(2,1)S(1)}, u32[]{:S(2)}, u32[]{:S(2)}) collective-permute-start(bf16[1,16,8,128]{3,2,1,0:T(8,128)(2,1)S(1)} %get-tuple-element.12), channel_id=1, source_target_pairs={{0,16},{16,32},{32,48},{48,64},{64,80},{80,96},{96,112},{112,128},... | collective-permute-start | bytes 98312 | tf_op jit(solution)/shard_map/ppermute | solution.py:12
  2.8 7.3 %collective-permute-start.1 = (bf16[1,16,8,128]{3,2,1,0:T(8,128)(2,1)S(1)}, bf16[1,16,8,128]{3,2,1,0:T(8,128)(2,1)S(1)}, u32[]{:S(2)}, u32[]{:S(2)}) collective-permute-start(bf16[1,16,8,128]{3,2,1,0:T(8,128)(2,1)S(1)} %get-tuple-element.11), channel_id=1, source_target_pairs={{16,0},{32,16},{48,32},{64,48},{80,64},{96,80},{112,96},{128,112},... | collective-permute-start | bytes 98312 | tf_op jit(solution)/shard_map/ppermute | solution.py:15
  10.2 6.2 %collective-permute-start.2 = (bf16[10,16,1,128]{3,2,1,0:T(2,128)(2,1)S(1)}, bf16[10,16,1,128]{3,2,1,0:T(2,128)(2,1)S(1)}, u32[]{:S(2)}, u32[]{:S(2)}) collective-permute-start(bf16[10,16,1,128]{3,2,1,0:T(2,128)(2,1)S(1)} %get-tuple-element.7), channel_id=1, source_target_pairs={{0,1},{1,2},{2,3},{3,4},{4,5},{5,6},{6,7},{7,8},{8,9},{9,10},{10,1... | collective-permute-start | bytes 122888 | tf_op jit(solution)/shard_map/ppermute | solution.py:12
  14.3 7.8 %collective-permute-start.3 = (bf16[10,16,1,128]{3,2,1,0:T(2,128)(2,1)S(1)}, bf16[10,16,1,128]{3,2,1,0:T(2,128)(2,1)S(1)}, u32[]{:S(2)}, u32[]{:S(2)}) collective-permute-start(bf16[10,16,1,128]{3,2,1,0:T(2,128)(2,1)S(1)} %get-tuple-element.8), channel_id=1, source_target_pairs={{1,0},{2,1},{3,2},{4,3},{5,4},{6,5},{7,6},{8,7},{9,8},{10,9},{11,1... | collective-permute-start | bytes 122888 | tf_op jit(solution)/shard_map/ppermute | solution.py:15
  27.3 9.0 %copy-start.2 = (pred[8,17]{0,1:T(8,128)(4,1)S(1)}, pred[8,17]{0,1:T(8,128)(4,1)}, u32[]{:S(2)}) copy-start(pred[8,17]{0,1:T(8,128)(4,1)} %constant.44) | copy-start | bytes 412
  46.7 22.5 %copy-start.1 = (bf16[64,864]{1,0:T(8,128)(2,1)S(1)}, bf16[64,864]{1,0:T(8,128)(2,1)}, u32[]{:S(2)}) copy-start(bf16[64,864]{1,0:T(8,128)(2,1)} %param.6) | copy-start | bytes 331780
  51.9 7.7 %collective-permute-start.4 = (bf16[1,32,4,64]{1,2,3,0:T(4,128)(2,1)S(1)}, bf16[1,32,4,64]{1,2,3,0:T(4,128)(2,1)S(1)}, u32[]{:S(2)}, u32[]{:S(2)}) collective-permute-start(bf16[1,32,4,64]{1,2,3,0:T(4,128)(2,1)S(1)} %get-tuple-element.9), channel_id=1, source_target_pairs={{0,16},{16,32},{32,48},{48,64},{64,80},{80,96},{96,112},{112,128},... | collective-permute-start | bytes 49160 | tf_op jit(solution)/shard_map/ppermute | solution.py:12
  53.8 7.6 %collective-permute-start.5 = (bf16[1,32,4,64]{1,2,3,0:T(4,128)(2,1)S(1)}, bf16[1,32,4,64]{1,2,3,0:T(4,128)(2,1)S(1)}, u32[]{:S(2)}, u32[]{:S(2)}) collective-permute-start(bf16[1,32,4,64]{1,2,3,0:T(4,128)(2,1)S(1)} %get-tuple-element.10), channel_id=1, source_target_pairs={{16,0},{32,16},{48,32},{64,48},{80,64},{96,80},{112,96},{128,112},... | collective-permute-start | bytes 49160 | tf_op jit(solution)/shard_map/ppermute | solution.py:15
  62.1 11.1 %collective-permute-start.6 = (bf16[6,32,1,64]{1,2,3,0:T(2,128)(2,1)S(1)}, bf16[6,32,1,64]{1,2,3,0:T(2,128)(2,1)S(1)}, u32[]{:S(2)}, u32[]{:S(2)}) collective-permute-start(bf16[6,32,1,64]{1,2,3,0:T(2,128)(2,1)S(1)} %get-tuple-element.5), channel_id=1, source_target_pairs={{0,1},{1,2},{2,3},{3,4},{4,5},{5,6},{6,7},{7,8},{8,9},{9,10},{10,1... | collective-permute-start | bytes 73736 | tf_op jit(solution)/shard_map/ppermute | solution.py:12
  67.9 9.1 %collective-permute-start.7 = (bf16[6,32,1,64]{1,2,3,0:T(2,128)(2,1)S(1)}, bf16[6,32,1,64]{1,2,3,0:T(2,128)(2,1)S(1)}, u32[]{:S(2)}, u32[]{:S(2)}) collective-permute-start(bf16[6,32,1,64]{1,2,3,0:T(2,128)(2,1)S(1)} %get-tuple-element.6), channel_id=1, source_target_pairs={{1,0},{2,1},{3,2},{4,3},{5,4},{6,5},{7,6},{8,7},{9,8},{10,9},{11,1... | collective-permute-start | bytes 73736 | tf_op jit(solution)/shard_map/ppermute | solution.py:15
  77.1 1.1 copy-start.3
  80.3 7.9 %collective-permute-start.8 = (bf16[1,64,2,32]{1,2,3,0:T(2,128)(2,1)S(1)}, bf16[1,64,2,32]{1,2,3,0:T(2,128)(2,1)S(1)}, u32[]{:S(2)}, u32[]{:S(2)}) collective-permute-start(bf16[1,64,2,32]{1,2,3,0:T(2,128)(2,1)S(1)} %get-tuple-element.13), channel_id=1, source_target_pairs={{0,16},{16,32},{32,48},{48,64},{64,80},{80,96},{96,112},{112,128},... | collective-permute-start | bytes 24584 | tf_op jit(solution)/shard_map/ppermute | solution.py:12
  82.2 7.2 %collective-permute-start.9 = (bf16[1,64,2,32]{1,2,3,0:T(2,128)(2,1)S(1)}, bf16[1,64,2,32]{1,2,3,0:T(2,128)(2,1)S(1)}, u32[]{:S(2)}, u32[]{:S(2)}) collective-permute-start(bf16[1,64,2,32]{1,2,3,0:T(2,128)(2,1)S(1)} %get-tuple-element.14), channel_id=1, source_target_pairs={{16,0},{32,16},{48,32},{64,48},{80,64},{96,80},{112,96},{128,112},... | collective-permute-start | bytes 24584 | tf_op jit(solution)/shard_map/ppermute | solution.py:15
  139.2 1.0 copy-start.4
where the time goes:
time: 145 us; the launch traced here: 144 us
  blocking collectives  48.7 us (34%)
  starting transfers between devices  35.4 us (24%)
  local copies, waits for them, and re-layouts  24.6 us (17%)
  waiting for transfers between devices  16.5 us (11%)
  matrix products  11.3 us (8%)
  other arithmetic  7.46 us (5%)
    all_gather x1, blocking collectives, per_device(): whole = lax.all_gather(grown, 'yz', axis=2, tiled=True)  48.7 us
    ppermute x5, starting transfers between devices, with_halo(): lax.ppermute(lax.slice_in_dim(block, 0, width, axis=dim), axis, backward)  19.8 us
    ppermute x5, starting transfers between devices, with_halo(): lax.ppermute(lax.slice_in_dim(block, block.shape[dim] - width, None, axis...  15.5 us
    conv_general_dilated x7, local copies, waits for them, and re-layouts, block_conv(): lax.conv_general_dilated(padded[None], kernel, (1, 1, 1), 'VALID', dimens...  13.2 us
    ppermute x5, waiting for transfers between devices, with_halo(): lax.ppermute(lax.slice_in_dim(block, 0, width, axis=dim), axis, backward)  12.9 us
    conv_general_dilated x3, matrix products, block_conv(): lax.conv_general_dilated(padded[None], kernel, (1, 1, 1), 'VALID', dimens...  11.3 us
    reduce_sum x2, other arithmetic, conv_pool(): return (jnp.sum(grouped, axis=(1, 4, 6)) * 0.125).astype(jnp.bfloat16)  5.47 us
    ppermute x5, waiting for transfers between devices, with_halo(): lax.ppermute(lax.slice_in_dim(block, block.shape[dim] - width, None, axis...  3.6 us
  transfers between devices with their start and end apart: 10, of which 6 were waited for; matrix products, arithmetic and copies ran while one was open for 2% of the time, Pallas kernels for 0%

commit v1 on v0

--- a/solution.py
+++ b/solution.py
@@ -55,7 +55,15 @@
     shards = lax.axis_size("yz")
     out_rows = weight_three.shape[0] // shards
     grown = with_halo(pooled_two, (("gx", 0),), 1)
-    whole = lax.all_gather(grown, "yz", axis=2, tiled=True)
+    whole = jnp.concatenate(
+        lax.all_to_all(
+            jnp.stack([grown] * lax.axis_size("yz"), axis=0),
+            axis_name="yz",
+            split_axis=0,
+            concat_axis=0,
+        ),
+        2,
+    )
     whole = jnp.pad(whole, ((0, 0), (0, 0), (1, 1), (1, 1)))
     picked = lax.dynamic_slice_in_dim(weight_three, lax.axis_index("yz") * out_rows, out_rows, 0)
     summed = jnp.moveaxis(conv_planes(whole, picked), 0, 1)

time: 145 us -> 128 us (0.88)
  the two profiles are of different devices: /device:TPU:2 before, /device:TPU:25 now
where the time goes in v1:
time: 128 us; the launch traced here: 127 us
  waiting for transfers between devices  42.3 us (33%)
  starting transfers between devices  38.9 us (30%)
  local copies, waits for them, and re-layouts  27 us (21%)
  matrix products  11.3 us (9%)
  other arithmetic  7.46 us (6%)
    ppermute x5, waiting for transfers between devices, with_halo(): lax.ppermute(lax.slice_in_dim(block, 0, width, axis=dim), axis, backward)  21.1 us
    ppermute x5, starting transfers between devices, with_halo(): lax.ppermute(lax.slice_in_dim(block, block.shape[dim] - width, None, axis...  19.2 us
    all_to_all x1, waiting for transfers between devices, per_device(): lax.all_to_all(jnp.stack([grown] * lax.axis_size('yz'), axis=0), axis_nam...  16.3 us
    conv_general_dilated x7, local copies, waits for them, and re-layouts, block_conv(): lax.conv_general_dilated(padded[None], kernel, (1, 1, 1), 'VALID', dimens...  13.2 us
    conv_general_dilated x3, matrix products, block_conv(): lax.conv_general_dilated(padded[None], kernel, (1, 1, 1), 'VALID', dimens...  11.3 us
    all_to_all x1, starting transfers between devices, per_device(): lax.all_to_all(jnp.stack([grown] * lax.axis_size('yz'), axis=0), axis_nam...  11.3 us
    ppermute x5, starting transfers between devices, with_halo(): lax.ppermute(lax.slice_in_dim(block, 0, width, axis=dim), axis, backward)  8.35 us
    reduce_sum x2, other arithmetic, conv_pool(): return (jnp.sum(grouped, axis=(1, 4, 6)) * 0.125).astype(jnp.bfloat16)  5.47 us
  transfers between devices with their start and end apart: 11, of which 7 were waited for; matrix products, arithmetic and copies ran while one was open for 2% of the time, Pallas kernels for 0%

profile of v1, /device:TPU:25, one launch (start us, length us, event | category | flops | bytes accessed | tf_op | source)
XLA Modules:
  0.0 127.4 jit_solution(8145035094760275544)
XLA Ops:
  0.0 0.8 fusion.64
  0.8 3.3 %collective-permute-start = (bf16[1,16,8,128]{3,2,1,0:T(8,128)(2,1)S(1)}, bf16[1,16,8,128]{3,2,1,0:T(8,128)(2,1)S(1)}, u32[]{:S(2)}, u32[]{:S(2)}) collective-permute-start(bf16[1,16,8,128]{3,2,1,0:T(8,128)(2,1)S(1)} %get-tuple-element.12), channel_id=1, source_target_pairs={{0,16},{16,32},{32,48},{48,64},{64,80},{80,96},{96,112},{112,128},... | collective-permute-start | bytes 98312 | tf_op jit(solution)/shard_map/ppermute | solution.py:12
  4.2 1.9 %collective-permute-start.1 = (bf16[1,16,8,128]{3,2,1,0:T(8,128)(2,1)S(1)}, bf16[1,16,8,128]{3,2,1,0:T(8,128)(2,1)S(1)}, u32[]{:S(2)}, u32[]{:S(2)}) collective-permute-start(bf16[1,16,8,128]{3,2,1,0:T(8,128)(2,1)S(1)} %get-tuple-element.11), channel_id=1, source_target_pairs={{16,0},{32,16},{48,32},{64,48},{80,64},{96,80},{112,96},{128,112},... | collective-permute-start | bytes 98312 | tf_op jit(solution)/shard_map/ppermute | solution.py:15
  6.1 1.0 constant_dynamic-update-slice_fusion.1
  7.1 4.4 %collective-permute-done.1 = bf16[1,16,8,128]{3,2,1,0:T(8,128)(2,1)S(1)} collective-permute-done((bf16[1,16,8,128]{3,2,1,0:T(8,128)(2,1)S(1)}, bf16[1,16,8,128]{3,2,1,0:T(8,128)(2,1)S(1)}, u32[]{:S(2)}, u32[]{:S(2)}) %collective-permute-start.1) | collective-permute-done | bytes 32800 | tf_op jit(solution)/shard_map/ppermute | solution.py:15
  11.6 4.4 %collective-permute-start.2 = (bf16[10,16,1,128]{3,2,1,0:T(2,128)(2,1)S(1)}, bf16[10,16,1,128]{3,2,1,0:T(2,128)(2,1)S(1)}, u32[]{:S(2)}, u32[]{:S(2)}) collective-permute-start(bf16[10,16,1,128]{3,2,1,0:T(2,128)(2,1)S(1)} %get-tuple-element.7), channel_id=1, source_target_pairs={{0,1},{1,2},{2,3},{3,4},{4,5},{5,6},{6,7},{7,8},{8,9},{9,10},{10,1... | collective-permute-start | bytes 122888 | tf_op jit(solution)/shard_map/ppermute | solution.py:12
  16.0 1.3 %collective-permute-start.3 = (bf16[10,16,1,128]{3,2,1,0:T(2,128)(2,1)S(1)}, bf16[10,16,1,128]{3,2,1,0:T(2,128)(2,1)S(1)}, u32[]{:S(2)}, u32[]{:S(2)}) collective-permute-start(bf16[10,16,1,128]{3,2,1,0:T(2,128)(2,1)S(1)} %get-tuple-element.8), channel_id=1, source_target_pairs={{1,0},{2,1},{3,2},{4,3},{5,4},{6,5},{7,6},{8,7},{9,8},{10,9},{11,1... | collective-permute-start | bytes 122888 | tf_op jit(solution)/shard_map/ppermute | solution.py:15
  17.3 0.9 copy.62
  18.2 4.5 %collective-permute-done.3 = bf16[10,16,1,128]{3,2,1,0:T(2,128)(2,1)S(1)} collective-permute-done((bf16[10,16,1,128]{3,2,1,0:T(2,128)(2,1)S(1)}, bf16[10,16,1,128]{3,2,1,0:T(2,128)(2,1)S(1)}, u32[]{:S(2)}, u32[]{:S(2)}) %collective-permute-start.3) | collective-permute-done | bytes 40992 | tf_op jit(solution)/shard_map/ppermute | solution.py:15
  22.7 1.2 fusion.35
  24.2 3.7 %reshape.69 = bf16[10,16,10,1,8,17]{5,4,2,1,0,3:T(8,128)(2,1)} reshape(bf16[10,16,10,1,136]{4,2,1,0,3:T(8,128)(2,1)S(1)} %pad.15) | data formatting | bytes 870400 | tf_op jit(solution)/shard_map/conv_general_dilated | solution.py:23
  27.9 7.9 %copy.61 = bf16[10,16,10,1,8,17]{1,4,5,2,0,3:T(8,128)(2,1)} copy(bf16[10,16,10,1,8,17]{5,4,2,1,0,3:T(8,128)(2,1)} %reshape.69) | data formatting | bytes 870400 | tf_op jit(solution)/shard_map/conv_general_dilated | solution.py:23
  35.8 1.1 slice.48
  37.0 7.3 %select_maximum_fusion = f32[8,8,8,17,32]{4,2,3,1,0:T(8,128)S(1)} fusion(pred[8,17]{0,1:T(8,128)(4,1)S(1)} %copy-done.2, bf16[32,3,3,3,16]{0,4,3,2,1:T(8,128)(2,1)S(1)} %bitcast.65, bf16[10,16,10,1,7,2]{1,4,5,2,0,3:T(8,128)(2,1)S(1)} %slice.48, bf16[10,16,10,1,8,17]{1,4,5,2,0,3:T(8,128)(2,1)} %copy.61), kind=kOutput, calls=%fused_computation.2 | convolution fusion | flops 242664448 | bytes 1621896 | tf_op jit(solution)/shard_map/conv_general_dilated | solution.py:23
  44.2 0.8 copy.63
  45.0 2.2 %slice.49 = f32[8,8,1,128,32]{4,1,3,0,2:T(8,128)} slice(f32[8,8,1,136,32]{4,1,3,0,2:T(8,128)S(1)} %bitcast.53), slice={[0:8], [0:8], [0:1], [0:128], [0:32]} | slice | bytes 2097152 | tf_op jit(solution)/shard_map/jit(relu)/max | solution.py:35
  47.3 5.0 %reduce_sum.18 = f32[4,32,4,64]{1,2,3,0:T(4,128)S(1)} reduce(f32[4,2,32,4,2,64,2]{2,4,3,6,5,1,0:T(2,128)} %bitcast.54, f32[]{:T(128)} %constant.8.clone.1), dimensions={1,4,6}, to_apply=%region_0.1 | reduce | flops 229376 | bytes 1179652 | tf_op jit(solution)/shard_map/reduce_sum | solution.py:38
  52.5 2.7 %collective-permute-start.4 = (bf16[1,32,4,64]{1,2,3,0:T(4,128)(2,1)S(1)}, bf16[1,32,4,64]{1,2,3,0:T(4,128)(2,1)S(1)}, u32[]{:S(2)}, u32[]{:S(2)}) collective-permute-start(bf16[1,32,4,64]{1,2,3,0:T(4,128)(2,1)S(1)} %get-tuple-element.9), channel_id=1, source_target_pairs={{0,16},{16,32},{32,48},{48,64},{64,80},{80,96},{96,112},{112,128},... | collective-permute-start | bytes 49160 | tf_op jit(solution)/shard_map/ppermute | solution.py:12
  55.2 1.9 %collective-permute-start.5 = (bf16[1,32,4,64]{1,2,3,0:T(4,128)(2,1)S(1)}, bf16[1,32,4,64]{1,2,3,0:T(4,128)(2,1)S(1)}, u32[]{:S(2)}, u32[]{:S(2)}) collective-permute-start(bf16[1,32,4,64]{1,2,3,0:T(4,128)(2,1)S(1)} %get-tuple-element.10), channel_id=1, source_target_pairs={{16,0},{32,16},{48,32},{64,48},{80,64},{96,80},{112,96},{128,112},... | collective-permute-start | bytes 49160 | tf_op jit(solution)/shard_map/ppermute | solution.py:15
  57.2 5.8 %collective-permute-done.5 = bf16[1,32,4,64]{1,2,3,0:T(4,128)(2,1)S(1)} collective-permute-done((bf16[1,32,4,64]{1,2,3,0:T(4,128)(2,1)S(1)}, bf16[1,32,4,64]{1,2,3,0:T(4,128)(2,1)S(1)}, u32[]{:S(2)}, u32[]{:S(2)}) %collective-permute-start.5) | collective-permute-done | bytes 16416 | tf_op jit(solution)/shard_map/ppermute | solution.py:15
  63.6 6.1 %collective-permute-start.6 = (bf16[6,32,1,64]{1,2,3,0:T(2,128)(2,1)S(1)}, bf16[6,32,1,64]{1,2,3,0:T(2,128)(2,1)S(1)}, u32[]{:S(2)}, u32[]{:S(2)}) collective-permute-start(bf16[6,32,1,64]{1,2,3,0:T(2,128)(2,1)S(1)} %get-tuple-element.5), channel_id=1, source_target_pairs={{0,1},{1,2},{2,3},{3,4},{4,5},{5,6},{6,7},{7,8},{8,9},{9,10},{10,1... | collective-permute-start | bytes 73736 | tf_op jit(solution)/shard_map/ppermute | solution.py:12
  69.7 1.3 %collective-permute-start.7 = (bf16[6,32,1,64]{1,2,3,0:T(2,128)(2,1)S(1)}, bf16[6,32,1,64]{1,2,3,0:T(2,128)(2,1)S(1)}, u32[]{:S(2)}, u32[]{:S(2)}) collective-permute-start(bf16[6,32,1,64]{1,2,3,0:T(2,128)(2,1)S(1)} %get-tuple-element.6), channel_id=1, source_target_pairs={{1,0},{2,1},{3,2},{4,3},{5,4},{6,5},{7,6},{8,7},{9,8},{10,9},{11,1... | collective-permute-start | bytes 73736 | tf_op jit(solution)/shard_map/ppermute | solution.py:15
  71.4 4.9 %collective-permute-done.6 = bf16[6,32,1,64]{1,2,3,0:T(2,128)(2,1)S(1)} collective-permute-done((bf16[6,32,1,64]{1,2,3,0:T(2,128)(2,1)S(1)}, bf16[6,32,1,64]{1,2,3,0:T(2,128)(2,1)S(1)}, u32[]{:S(2)}, u32[]{:S(2)}) %collective-permute-start.6) | collective-permute-done | bytes 24608 | tf_op jit(solution)/shard_map/ppermute | solution.py:12
  76.4 1.2 collective-permute-done.7
  78.8 1.4 %fusion.36 = f32[4,4,8,9,64]{4,2,3,1,0:T(8,128)S(1)} fusion(bf16[64,3,3,3,32]{0,4,3,2,1:T(8,128)(2,1)S(1)} %bitcast.63, bf16[6,32,6,1,7,2]{1,4,5,2,0,3:T(8,128)(2,1)S(1)} %slice.54, bf16[6,32,6,1,8,9]{1,4,5,2,0,3:T(8,128)(2,1)S(1)} %copy.69, pred[8,9]{0,1:T(8,128)(4,1)S(1)} %copy-done.3), kind=kOutput, calls=%fused_computation.34 | convolution fusion | flops 128157696 | bytes 603720 | tf_op jit(solution)/shard_map/conv_general_dilated | solution.py:23
  80.9 2.7 %collective-permute-start.8 = (bf16[1,64,2,32]{1,2,3,0:T(2,128)(2,1)S(1)}, bf16[1,64,2,32]{1,2,3,0:T(2,128)(2,1)S(1)}, u32[]{:S(2)}, u32[]{:S(2)}) collective-permute-start(bf16[1,64,2,32]{1,2,3,0:T(2,128)(2,1)S(1)} %get-tuple-element.13), channel_id=1, source_target_pairs={{0,16},{16,32},{32,48},{48,64},{64,80},{80,96},{96,112},{112,128},... | collective-permute-start | bytes 24584 | tf_op jit(solution)/shard_map/ppermute | solution.py:12
  83.7 1.9 %collective-permute-start.9 = (bf16[1,64,2,32]{1,2,3,0:T(2,128)(2,1)S(1)}, bf16[1,64,2,32]{1,2,3,0:T(2,128)(2,1)S(1)}, u32[]{:S(2)}, u32[]{:S(2)}) collective-permute-start(bf16[1,64,2,32]{1,2,3,0:T(2,128)(2,1)S(1)} %get-tuple-element.14), channel_id=1, source_target_pairs={{16,0},{32,16},{48,32},{64,48},{80,64},{96,80},{112,96},{128,112},... | collective-permute-start | bytes 24584 | tf_op jit(solution)/shard_map/ppermute | solution.py:15
  85.6 5.2 %collective-permute-done.9 = bf16[1,64,2,32]{1,2,3,0:T(2,128)(2,1)S(1)} collective-permute-done((bf16[1,64,2,32]{1,2,3,0:T(2,128)(2,1)S(1)}, bf16[1,64,2,32]{1,2,3,0:T(2,128)(2,1)S(1)}, u32[]{:S(2)}, u32[]{:S(2)}) %collective-permute-start.9) | collective-permute-done | bytes 8224 | tf_op jit(solution)/shard_map/ppermute | solution.py:15
  91.2 1.5 %reshape.70 = bf16[16,2,8192]{2,1,0:T(2,128)(2,1)} reshape(bf16[16,4,2,32,64]{4,3,2,1,0:T(8,128)(2,1)S(1)} %broadcast_bitcast_fusion) | data formatting | bytes 1048576
  92.7 11.3 %all-to-all-start = ((bf16[16,2,8192]{2,1,0:T(2,128)(2,1)}), bf16[16,2,8192]{2,1,0:T(2,128)(2,1)S(1)}, u32[]{:S(2)}, u32[]{:S(2)}) async-start(bf16[16,2,8192]{2,1,0:T(2,128)(2,1)} %reshape.70), calls=%async_computation | async-start | bytes 1048576 | tf_op jit(solution)/shard_map/all_to_all | solution.py:59
  104.2 16.3 %all-to-all-done = bf16[16,2,8192]{2,1,0:T(2,128)(2,1)S(1)} async-done(((bf16[16,2,8192]{2,1,0:T(2,128)(2,1)}), bf16[16,2,8192]{2,1,0:T(2,128)(2,1)S(1)}, u32[]{:S(2)}, u32[]{:S(2)}) %all-to-all-start) | async-done | bytes 524320 | tf_op jit(solution)/shard_map/all_to_all | solution.py:59
  123.3 2.7 %fusion.30 = bf16[2,32,8,5,8]{4,2,3,1,0:T(8,128)(2,1)S(1)} fusion(bf16[8,3,3,3,64]{0,4,3,2,1:T(8,128)(2,1)S(1)} %bitcast.62, bf16[4,64,34,1,7,2]{1,4,5,2,0,3:T(8,128)(2,1)S(1)} %slice.58, bf16[4,64,34,1,8,5]{1,4,5,2,0,3:T(8,128)(2,1)S(1)} %copy.76, pred[8,5]{0,1:T(8,128)(4,1)S(1)} %copy-done.4), kind=kOutput, calls=%fused_computation.29 | convolution fusion | flops 73764864 | bytes 1008680 | tf_op jit(solution)/shard_map/conv_general_dilated | solution.py:23
  (52 shorter events, 8.3 us)
Async XLA Ops:
  0.0 104.1 %copy-start = (bf16[128,1728]{0,1:T(8,128)(2,1)S(1)}, bf16[128,1728]{0,1:T(8,128)(2,1)}, u32[]{:S(2)}) copy-start(bf16[128,1728]{0,1:T(8,128)(2,1)} %param.7) | copy-start | bytes 1327108
  0.8 5.3 %collective-permute-start = (bf16[1,16,8,128]{3,2,1,0:T(8,128)(2,1)S(1)}, bf16[1,16,8,128]{3,2,1,0:T(8,128)(2,1)S(1)}, u32[]{:S(2)}, u32[]{:S(2)}) collective-permute-start(bf16[1,16,8,128]{3,2,1,0:T(8,128)(2,1)S(1)} %get-tuple-element.12), channel_id=1, source_target_pairs={{0,16},{16,32},{32,48},{48,64},{64,80},{80,96},{96,112},{112,128},... | collective-permute-start | bytes 98312 | tf_op jit(solution)/shard_map/ppermute | solution.py:12
  4.2 7.3 %collective-permute-start.1 = (bf16[1,16,8,128]{3,2,1,0:T(8,128)(2,1)S(1)}, bf16[1,16,8,128]{3,2,1,0:T(8,128)(2,1)S(1)}, u32[]{:S(2)}, u32[]{:S(2)}) collective-permute-start(bf16[1,16,8,128]{3,2,1,0:T(8,128)(2,1)S(1)} %get-tuple-element.11), channel_id=1, source_target_pairs={{16,0},{32,16},{48,32},{64,48},{80,64},{96,80},{112,96},{128,112},... | collective-permute-start | bytes 98312 | tf_op jit(solution)/shard_map/ppermute | solution.py:15
  11.6 6.6 %collective-permute-start.2 = (bf16[10,16,1,128]{3,2,1,0:T(2,128)(2,1)S(1)}, bf16[10,16,1,128]{3,2,1,0:T(2,128)(2,1)S(1)}, u32[]{:S(2)}, u32[]{:S(2)}) collective-permute-start(bf16[10,16,1,128]{3,2,1,0:T(2,128)(2,1)S(1)} %get-tuple-element.7), channel_id=1, source_target_pairs={{0,1},{1,2},{2,3},{3,4},{4,5},{5,6},{6,7},{7,8},{8,9},{9,10},{10,1... | collective-permute-start | bytes 122888 | tf_op jit(solution)/shard_map/ppermute | solution.py:12
  16.0 6.7 %collective-permute-start.3 = (bf16[10,16,1,128]{3,2,1,0:T(2,128)(2,1)S(1)}, bf16[10,16,1,128]{3,2,1,0:T(2,128)(2,1)S(1)}, u32[]{:S(2)}, u32[]{:S(2)}) collective-permute-start(bf16[10,16,1,128]{3,2,1,0:T(2,128)(2,1)S(1)} %get-tuple-element.8), channel_id=1, source_target_pairs={{1,0},{2,1},{3,2},{4,3},{5,4},{6,5},{7,6},{8,7},{9,8},{10,9},{11,1... | collective-permute-start | bytes 122888 | tf_op jit(solution)/shard_map/ppermute | solution.py:15
  27.9 9.0 %copy-start.2 = (pred[8,17]{0,1:T(8,128)(4,1)S(1)}, pred[8,17]{0,1:T(8,128)(4,1)}, u32[]{:S(2)}) copy-start(pred[8,17]{0,1:T(8,128)(4,1)} %constant.44) | copy-start | bytes 412
  47.3 23.7 %copy-start.1 = (bf16[64,864]{1,0:T(8,128)(2,1)S(1)}, bf16[64,864]{1,0:T(8,128)(2,1)}, u32[]{:S(2)}) copy-start(bf16[64,864]{1,0:T(8,128)(2,1)} %param.6) | copy-start | bytes 331780
  52.5 4.7 %collective-permute-start.4 = (bf16[1,32,4,64]{1,2,3,0:T(4,128)(2,1)S(1)}, bf16[1,32,4,64]{1,2,3,0:T(4,128)(2,1)S(1)}, u32[]{:S(2)}, u32[]{:S(2)}) collective-permute-start(bf16[1,32,4,64]{1,2,3,0:T(4,128)(2,1)S(1)} %get-tuple-element.9), channel_id=1, source_target_pairs={{0,16},{16,32},{32,48},{48,64},{64,80},{80,96},{96,112},{112,128},... | collective-permute-start | bytes 49160 | tf_op jit(solution)/shard_map/ppermute | solution.py:12
  55.2 7.7 %collective-permute-start.5 = (bf16[1,32,4,64]{1,2,3,0:T(4,128)(2,1)S(1)}, bf16[1,32,4,64]{1,2,3,0:T(4,128)(2,1)S(1)}, u32[]{:S(2)}, u32[]{:S(2)}) collective-permute-start(bf16[1,32,4,64]{1,2,3,0:T(4,128)(2,1)S(1)} %get-tuple-element.10), channel_id=1, source_target_pairs={{16,0},{32,16},{48,32},{64,48},{80,64},{96,80},{112,96},{128,112},... | collective-permute-start | bytes 49160 | tf_op jit(solution)/shard_map/ppermute | solution.py:15
  63.6 12.7 %collective-permute-start.6 = (bf16[6,32,1,64]{1,2,3,0:T(2,128)(2,1)S(1)}, bf16[6,32,1,64]{1,2,3,0:T(2,128)(2,1)S(1)}, u32[]{:S(2)}, u32[]{:S(2)}) collective-permute-start(bf16[6,32,1,64]{1,2,3,0:T(2,128)(2,1)S(1)} %get-tuple-element.5), channel_id=1, source_target_pairs={{0,1},{1,2},{2,3},{3,4},{4,5},{5,6},{6,7},{7,8},{8,9},{9,10},{10,1... | collective-permute-start | bytes 73736 | tf_op jit(solution)/shard_map/ppermute | solution.py:12
  69.7 7.9 %collective-permute-start.7 = (bf16[6,32,1,64]{1,2,3,0:T(2,128)(2,1)S(1)}, bf16[6,32,1,64]{1,2,3,0:T(2,128)(2,1)S(1)}, u32[]{:S(2)}, u32[]{:S(2)}) collective-permute-start(bf16[6,32,1,64]{1,2,3,0:T(2,128)(2,1)S(1)} %get-tuple-element.6), channel_id=1, source_target_pairs={{1,0},{2,1},{3,2},{4,3},{5,4},{6,5},{7,6},{8,7},{9,8},{10,9},{11,1... | collective-permute-start | bytes 73736 | tf_op jit(solution)/shard_map/ppermute | solution.py:15
  77.7 1.1 copy-start.3
  80.9 4.6 %collective-permute-start.8 = (bf16[1,64,2,32]{1,2,3,0:T(2,128)(2,1)S(1)}, bf16[1,64,2,32]{1,2,3,0:T(2,128)(2,1)S(1)}, u32[]{:S(2)}, u32[]{:S(2)}) collective-permute-start(bf16[1,64,2,32]{1,2,3,0:T(2,128)(2,1)S(1)} %get-tuple-element.13), channel_id=1, source_target_pairs={{0,16},{16,32},{32,48},{48,64},{64,80},{80,96},{96,112},{112,128},... | collective-permute-start | bytes 24584 | tf_op jit(solution)/shard_map/ppermute | solution.py:12
  83.7 7.2 %collective-permute-start.9 = (bf16[1,64,2,32]{1,2,3,0:T(2,128)(2,1)S(1)}, bf16[1,64,2,32]{1,2,3,0:T(2,128)(2,1)S(1)}, u32[]{:S(2)}, u32[]{:S(2)}) collective-permute-start(bf16[1,64,2,32]{1,2,3,0:T(2,128)(2,1)S(1)} %get-tuple-element.14), channel_id=1, source_target_pairs={{16,0},{32,16},{48,32},{64,48},{80,64},{96,80},{112,96},{128,112},... | collective-permute-start | bytes 24584 | tf_op jit(solution)/shard_map/ppermute | solution.py:15
  92.7 27.8 %all-to-all-start = ((bf16[16,2,8192]{2,1,0:T(2,128)(2,1)}), bf16[16,2,8192]{2,1,0:T(2,128)(2,1)S(1)}, u32[]{:S(2)}, u32[]{:S(2)}) async-start(bf16[16,2,8192]{2,1,0:T(2,128)(2,1)} %reshape.70), calls=%async_computation | async-start | bytes 1048576 | tf_op jit(solution)/shard_map/all_to_all | solution.py:59
  122.2 1.0 copy-start.4
